TPU v7x, 32 devices: a whole 2x2x4 slice. The times are simulated.
32 devices in a mesh: loop: 8 (over y, x, core), tp: 4 (over z).
Axes of the slice: x: 2, y: 2, z: 4, core: 2. Of those that a mesh axis runs over, the one named last changes fastest.
Arguments:
- tokens: bfloat16 [2048, 4096], P('loop', 'tp'), may hold values from -6 to 6
- out_grad: bfloat16 [2048, 6144], P('loop', 'tp'), may hold values from -6 to 6
- qkv_weight: bfloat16 [3, 4096, 6144], P(None, 'loop', 'tp'), may hold values from -0.09375 to 0.09375
- dest_row: int32 [2048], P('loop'), may hold values from 0 to 383, as said below
- loop_modality: int32 [8], replicated, may hold values from 0 to 2, as said below
Outputs:
- projected: bfloat16 [2048, 6144], P('loop', 'tp')
- input_grad: bfloat16 [2048, 4096], P('loop', 'tp')
- weight_grad: bfloat16 [3, 4096, 6144], P(None, 'loop', 'tp')
Inputs may be any that keep to these rules, and one draw needn't show every extreme that they name: `dest_row`: within each aligned block of 256 tokens the values are distinct, so at most 48 tokens of one block name one loop; in every draw some loop is named by exactly 48 tokens of every block. `loop_modality`: A quarter of the loops hold 0, half hold 1, a quarter hold 2.
All inputs are finite; a program needn't handle non-finite values.
Results may differ from a plain program's by a relative error of at most 0.014.
Values may be sent and summed in bfloat16 or wider, within the bound.
No kernel may reach another device: no remote copies, remote signals or barrier semaphores. Data moves between devices by JAX's collectives and lax.ppermute only.
A program may use at most 128 MiB of HBM per device.

v0:
```python
import math
import jax
import jax.numpy as jnp
from jax import lax
from jax.sharding import PartitionSpec as P


def per_device(tokens, out_grad, qkv_weight, dest_row, loop_modality):
    loop_count = lax.axis_size("loop")
    row_count, feature_part = tokens.shape
    kinds, block_rows, column_count = qkv_weight.shape
    capacity = 3 * row_count // (2 * loop_count)
    grad_scale = 1.0 / math.sqrt(row_count * loop_count)
    own_kind = loop_modality[dest_row // capacity]
    kind_of = lax.all_gather(own_kind, "loop", axis=0, tiled=True)
    grads = lax.all_gather(out_grad, "loop", axis=0, tiled=True)
    features = lax.all_gather(tokens, "tp", axis=1, tiled=True)
    rows = lax.all_to_all(features, "loop", split_axis=1, concat_axis=0, tiled=True)
    masks = [(kind_of == kind)[:, None] for kind in range(kinds)]
    term = sum(
        (
            lax.dot_general(
                jnp.where(masks[kind], grads, 0),
                qkv_weight[kind],
                (((1,), (1,)), ((), ())),
                preferred_element_type=jnp.float32,
            )
            for kind in range(kinds)
        )
    ).astype(jnp.bfloat16)
    term = lax.all_to_all(term, "loop", split_axis=0, concat_axis=1, tiled=True)
    input_grad = lax.psum_scatter(term, "tp", scatter_dimension=1, tiled=True)
    partial = sum(
        (
            jnp.dot(
                jnp.where(masks[kind], rows, 0),
                qkv_weight[kind],
                preferred_element_type=jnp.float32,
            )
            for kind in range(kinds)
        )
    ).astype(jnp.bfloat16)
    projected = lax.psum_scatter(partial, "loop", scatter_dimension=0, tiled=True)
    weight_grad = jnp.stack(
        [
            (
                lax.dot_general(
                    jnp.where(masks[kind], rows, 0),
                    grads,
                    (((0,), (0,)), ((), ())),
                    preferred_element_type=jnp.float32,
                )
                * grad_scale
            ).astype(jnp.bfloat16)
            for kind in range(kinds)
        ]
    )
    return (projected, input_grad, weight_grad)


def solution(mesh):
    placed = (P("loop", "tp"), P("loop", "tp"), P(None, "loop", "tp"), P("loop"), P())
    return jax.shard_map(
        per_device,
        mesh=mesh,
        in_specs=placed,
        out_specs=(P("loop", "tp"), P("loop", "tp"), P(None, "loop", "tp")),
        check_vma=False,
    )
```

profile of v0, /device:TPU:0, one launch (start us, length us, event | category | flops | bytes accessed | tf_op | source)
XLA Modules:
  0.0 278.5 jit_solution(15667492491029857206)
XLA Ops:
  7.2 0.0 copy-start.2
  7.2 0.0 copy-start.3
  7.2 0.0 all-gather.5.cloned.1.call-start
  7.2 2.0 copy.17
  9.3 0.0 all-gather.5.cloned.1.call-update
  9.3 0.0 all-gather.7.cloned.1.call-start
  9.3 0.7 all-gather.7.cloned.1.call-update
  10.0 48.5 %all-gather.5.cloned.1.call-done = bf16[256,4096]{0,1:T(8,128)(2,1)} async-done(((bf16[256,1024]{0,1:T(8,128)(2,1)}), bf16[256,4096]{0,1:T(8,128)(2,1)}) %all-gather.5.cloned.1.call-update) | async-done | bytes 2097168 | tf_op jit(solution)/shard_map/all_gather | solution.py:17
  58.5 3.7 %all-to-all-start = ((bf16[256,8,512]{0,2,1:T(8,128)(2,1)}), bf16[256,8,512]{0,2,1:T(8,128)(2,1)S(1)}, u32[]{:S(2)}, u32[]{:S(2)}) async-start(bf16[256,8,512]{0,2,1:T(8,128)(2,1)} %bitcast.68), calls=%async_computation | async-start | bytes 4194304 | tf_op jit(solution)/shard_map/all_to_all | solution.py:18
  62.2 0.0 reduce-scatter.3.cloned.1.call-start
  62.2 0.0 copy-done.2
  62.3 0.7 fusion.37
  62.9 0.0 copy-done.3
  63.0 5.2 %compare_select_fusion.1 = s32[256]{0:T(256)S(1)} fusion(s32[256]{0:T(256)S(1)} %copy-done.3, s32[]{:T(128)} %bitcast, s32[]{:T(128)} %bitcast.1, s32[]{:T(128)} %bitcast.2, s32[]{:T(128)} %bitcast.3, s32[]{:T(128)} %bitcast.4, s32[]{:T(128)} %bitcast.5, s32[]{:T(128)} %bitcast.6, s32[]{:T(128)} %bitcast.7), kind=kLoop, calls=%fused_computation.48 | loop fusion | flops 6400 | bytes 2080 | tf_op jit(solution)/shard_map/gather | solution.py:14
  68.1 32.2 %all-gather.1 = s32[8,1,256]{2,1,0:T(1,128)S(1)} all-gather(s32[1,1,256]{2,1,0:T(1,128)S(1)} %bitcast.75), channel_id=2, replica_groups=mesh['loop'=8,'tp'=4] {'loop'}, dimensions={0}, use_global_device_ids=true | all-gather | bytes 9216 | tf_op jit(solution)/shard_map/all_gather | solution.py:15
  100.3 0.0 all-to-all-done
  100.3 2.8 %broadcast_select_fusion = (bf16[8,256,512]{1,2,0:T(8,128)(2,1)}, bf16[8,256,512]{1,2,0:T(8,128)(2,1)}, bf16[8,256,512]{1,2,0:T(8,128)(2,1)}) fusion(pred[8,256]{1,0:T(8,128)(4,1)S(1)} %bitcast.72, bf16[256,8,512]{0,2,1:T(8,128)(2,1)S(1)} %all-to-all-done, pred[8,256]{1,0:T(8,128)(4,1)S(1)} %bitcast.74, pred[8,256]{1,0:T(8,128)(4,1)S(1)} %bitcast.73), kind=kLoop, calls=%fused_computation.27 | loop fusion | flops 3145728 | bytes 8394752 | tf_op jit(solution)/shard_map/jit(_where)/select_n | solution.py:36
  103.2 3.9 %copy.20 = bf16[8,256,512]{2,1,0:T(8,128)(2,1)} copy(bf16[8,256,512]{1,2,0:T(8,128)(2,1)} %get-tuple-element.8) | data formatting | bytes 4194304 | tf_op jit(solution)/shard_map/jit(_where)/select_n | solution.py:36
  107.1 4.0 %copy.18 = bf16[8,256,512]{2,1,0:T(8,128)(2,1)} copy(bf16[8,256,512]{1,2,0:T(8,128)(2,1)} %get-tuple-element.7) | data formatting | bytes 4194304 | tf_op jit(solution)/shard_map/jit(_where)/select_n | solution.py:36
  111.1 3.9 %copy.22 = bf16[8,256,512]{2,1,0:T(8,128)(2,1)} copy(bf16[8,256,512]{1,2,0:T(8,128)(2,1)} %get-tuple-element.6) | data formatting | bytes 4194304 | tf_op jit(solution)/shard_map/jit(_where)/select_n | solution.py:36
  115.0 0.0 copy-start.1
  115.0 10.2 %fusion.23 = f32[2048,1536]{1,0:T(8,128)} fusion(bf16[2048,512]{1,0:T(8,128)(2,1)} %bitcast.69, bf16[3,512,1536]{2,1,0:T(8,128)(2,1)} %param.7), kind=kOutput, calls=%fused_computation.33 | convolution fusion | flops 3221225472 | bytes 16252928 | tf_op jit(solution)/shard_map/dot_general | solution.py:35
  125.2 0.0 copy-done.1
  125.2 0.0 copy-start
  125.2 7.8 %fusion.26 = f32[2048,1536]{1,0:T(8,128)} fusion(bf16[2048,512]{1,0:T(8,128)(2,1)S(1)} %bitcast.70, bf16[3,512,1536]{2,1,0:T(8,128)(2,1)} %param.7), kind=kOutput, calls=%fused_computation.36 | convolution fusion | flops 3221225472 | bytes 16252928 | tf_op jit(solution)/shard_map/dot_general | solution.py:35
  133.0 0.0 copy-done
  133.0 13.3 %add_convert_fusion = bf16[2048,1536]{1,0:T(8,128)(2,1)} fusion(f32[2048,1536]{1,0:T(8,128)} %fusion.26, f32[2048,1536]{1,0:T(8,128)} %fusion.23, bf16[2048,512]{1,0:T(8,128)(2,1)S(1)} %bitcast.65, bf16[3,512,1536]{2,1,0:T(8,128)(2,1)} %param.7), kind=kOutput, calls=%fused_computation | convolution fusion | flops 3230662656 | bytes 35127296 | tf_op jit(solution)/shard_map/dot_general | solution.py:35
  146.3 0.0 reduce-scatter.3.cloned.1.call-update
  146.4 0.2 reduce-scatter.5.cloned.1.call-start
  146.6 0.0 all-gather.7.cloned.1.call-done
  146.7 0.0 copy-start.4
  146.7 6.3 %fusion = f32[2048,512]{1,0:T(8,128)S(1)} fusion(bf16[2048,1536]{1,0:T(8,128)(2,1)} %all-gather.7.cloned.1.call-done, pred[2048]{0:T(1024)(128)(4,1)S(1)} %reshape.57, bf16[3,512,1536]{2,1,0:T(8,128)(2,1)} %param.7), kind=kOutput, calls=%fused_computation.1 | convolution fusion | flops 3224371200 | bytes 12060672 | tf_op jit(solution)/shard_map/dot_general | solution.py:22
  153.0 0.0 copy-done.4
  153.0 5.2 %fusion.2 = f32[2048,512]{1,0:T(8,128)S(1)} fusion(bf16[2048,1536]{1,0:T(8,128)(2,1)S(1)} %copy-done.4, pred[2048]{0:T(1024)(128)(4,1)S(1)} %reshape.55, bf16[3,512,1536]{2,1,0:T(8,128)(2,1)} %param.7), kind=kOutput, calls=%fused_computation.3 | convolution fusion | flops 3224371200 | bytes 12060672 | tf_op jit(solution)/shard_map/dot_general | solution.py:22
  158.2 5.2 %add_convert_fusion.1 = bf16[2048,512]{1,0:T(8,128)(2,1)S(1)} fusion(f32[2048,512]{1,0:T(8,128)S(1)} %fusion, f32[2048,512]{1,0:T(8,128)S(1)} %fusion.2, bf16[2048,1536]{1,0:T(8,128)(2,1)S(1)} %copy-done.4, pred[2048]{0:T(1024)(128)(4,1)S(1)} %reshape.53, bf16[3,512,1536]{2,1,0:T(8,128)(2,1)} %param.7), kind=kOutput, calls=%fused_computation.11 | convolution fusion | flops 3227516928 | bytes 18352128 | tf_op jit(solution)/shard_map/dot_general | solution.py:22
  163.4 45.9 %all_to_all.38 = bf16[8,256,512]{2,1,0:T(8,128)(2,1)S(1)} all-to-all(bf16[8,256,512]{2,1,0:T(8,128)(2,1)S(1)} %bitcast.71), channel_id=1, replica_groups=mesh['loop'=8,'tp'=4] {'loop'}, dimensions={0} | all-to-all | bytes 4194304 | tf_op jit(solution)/shard_map/all_to_all | solution.py:31
  209.3 1.6 copy.25
  210.9 0.0 reduce-scatter.5.cloned.1.call-update
  210.9 2.4 copy.24
  213.3 3.7 %bitcast_select_fusion.2 = (bf16[2048,512]{1,0:T(8,128)(2,1)S(1)}, bf16[2048,512]{1,0:T(8,128)(2,1)S(1)}, bf16[2048,512]{1,0:T(8,128)(2,1)S(1)}) fusion(bf16[8,256,512]{2,1,0:T(8,128)(2,1)} %copy.24, pred[2048]{0:T(1024)(128)(4,1)S(1)} %reshape.53, pred[2048]{0:T(1024)(128)(4,1)S(1)} %reshape.55, pred[2048]{0:T(1024)(128)(4,1)S(1)} %reshape.57), kind=kLoop, calls=%fused_computation.26 | loop fusion | flops 3145728 | bytes 8394752 | tf_op jit(solution)/shard_map/jit(_where)/select_n | solution.py:36
  217.0 0.0 slice-start.1
  217.0 6.5 %fusion.15 = bf16[1,512,1536]{2,1,0:T(8,128)(2,1)S(1)} fusion(bf16[2048,512]{1,0:T(8,128)(2,1)S(1)} %get-tuple-element.5, bf16[2048,1536]{1,0:T(8,128)(2,1)} %all-gather.7.cloned.1.call-done), kind=kOutput, calls=%fused_computation.21 | convolution fusion | flops 3222798336 | bytes 9961472 | tf_op jit(solution)/shard_map/dot_general | solution.py:47
  223.5 0.0 slice-done
  223.5 0.0 slice-done.1
  223.5 3.6 %fusion.16 = bf16[1,512,1536]{2,1,0:T(8,128)(2,1)S(1)} fusion(bf16[2048,512]{1,0:T(8,128)(2,1)S(1)} %get-tuple-element.4, bf16[2048,1536]{1,0:T(8,128)(2,1)S(1)} %bitcast.77), kind=kOutput, calls=%fused_computation.22 | convolution fusion | flops 3222798336 | bytes 9961472 | tf_op jit(solution)/shard_map/dot_general | solution.py:47
  227.1 3.6 %fusion.17 = bf16[1,512,1536]{2,1,0:T(8,128)(2,1)S(1)} fusion(bf16[2048,512]{1,0:T(8,128)(2,1)S(1)} %get-tuple-element.3, bf16[2048,1536]{1,0:T(8,128)(2,1)S(1)} %bitcast.77), kind=kOutput, calls=%fused_computation.23 | convolution fusion | flops 3222798336 | bytes 9961472 | tf_op jit(solution)/shard_map/dot_general | solution.py:47
  230.7 2.5 pad_maximum_fusion
  233.2 38.8 %reduce-scatter.5.cloned.1.call-done = bf16[256,1024]{1,0:T(8,128)(2,1)} async-done(((bf16[256,4096]{1,0:T(8,128)(2,1)}), bf16[256,1024]{1,0:T(8,128)(2,1)}) %reduce-scatter.5.cloned.1.call-update) | async-done | bytes 524304 | tf_op jit(solution)/shard_map/reduce_scatter | solution.py:32
  (7 shorter events, 0.0 us)
Async XLA Ops:
  7.2 55.1 %copy-start.2 = (s32[8]{0:T(128)S(1)}, s32[8]{0:T(128)}, u32[]{:S(2)}) copy-start(s32[8]{0:T(128)} %param.9) | copy-start | bytes 100
  7.2 55.8 %copy-start.3 = (s32[256]{0:T(256)S(1)}, s32[256]{0:T(256)}, u32[]{:S(2)}) copy-start(s32[256]{0:T(256)} %param.8) | copy-start | bytes 3076
  7.2 51.4 %all-gather.5.cloned.1.call-start = ((), (), s32[]{:S(2)}) async-start(), calls=%async_computation.4 | async-start | bytes 2621440 | tf_op jit(solution)/shard_map/all_gather | solution.py:17
  9.3 137.4 %all-gather.7.cloned.1.call-start = ((), (), s32[]{:S(2)}) async-start(), calls=%async_computation.6 | async-start | bytes 7077888 | tf_op jit(solution)/shard_map/all_gather | solution.py:16
  58.5 41.8 %all-to-all-start = ((bf16[256,8,512]{0,2,1:T(8,128)(2,1)}), bf16[256,8,512]{0,2,1:T(8,128)(2,1)S(1)}, u32[]{:S(2)}, u32[]{:S(2)}) async-start(bf16[256,8,512]{0,2,1:T(8,128)(2,1)} %bitcast.68), calls=%async_computation | async-start | bytes 4194304 | tf_op jit(solution)/shard_map/all_to_all | solution.py:18
  62.2 171.0 %reduce-scatter.3.cloned.1.call-start = ((), (), s32[]{:S(2)}) async-start(), calls=%async_computation.5 | async-start | bytes 7077888 | tf_op jit(solution)/shard_map/reduce_scatter | solution.py:43
  115.0 10.2 %copy-start.1 = (bf16[8,256,512]{2,1,0:T(8,128)(2,1)S(1)}, bf16[8,256,512]{2,1,0:T(8,128)(2,1)}, u32[]{:S(2)}) copy-start(bf16[8,256,512]{2,1,0:T(8,128)(2,1)} %copy.18) | copy-start | bytes 6291460
  125.2 7.9 %copy-start = (bf16[8,256,512]{2,1,0:T(8,128)(2,1)S(1)}, bf16[8,256,512]{2,1,0:T(8,128)(2,1)}, u32[]{:S(2)}) copy-start(bf16[8,256,512]{2,1,0:T(8,128)(2,1)} %copy.22) | copy-start | bytes 6291460
  146.4 125.6 %reduce-scatter.5.cloned.1.call-start = ((), (), s32[]{:S(2)}) async-start(), calls=%async_computation.7 | async-start | bytes 2621440 | tf_op jit(solution)/shard_map/reduce_scatter | solution.py:32
  146.7 6.3 %copy-start.4 = (bf16[2048,1536]{1,0:T(8,128)(2,1)S(1)}, bf16[2048,1536]{1,0:T(8,128)(2,1)}, u32[]{:S(2)}) copy-start(bf16[2048,1536]{1,0:T(8,128)(2,1)} %all-gather.7.cloned.1.call-done) | copy-start | bytes 18874372
  213.3 10.2 %slice-start = ((s8[6291456]{0:T(1024)(128)(4,1)}), s8[4194304]{0:T(1024)(128)(4,1)S(1)}, s32[]{:S(2)}) async-start(s8[6291456]{0:T(1024)(128)(4,1)} %bitcast.76), calls=%async_computation.8 | async-start | bytes 8388608
  217.0 6.5 %slice-start.1 = ((s8[6291456]{0:T(1024)(128)(4,1)}), s8[2097152]{0:T(1024)(128)(4,1)S(1)}, s32[]{:S(2)}) async-start(s8[6291456]{0:T(1024)(128)(4,1)} %bitcast.76), calls=%async_computation.9 | async-start | bytes 4194304
Sparse Core Ops, SparseCore 0:
  10.1 48.3 all-gather.4
  60.4 58.3 all-gather.6
  146.5 79.0 reduce-scatter.2
  228.3 43.6 reduce-scatter.4
where the time goes:
time: 279 us
  waiting for transfers between devices  88.1 us (32%)
  blocking collectives  78.1 us (28%)
  matrix products  61.7 us (22%)
  local copies, waits for them, and re-layouts  18.6 us (7%)
  other arithmetic  14.1 us (5%)
  between operations  13.9 us (5%)
  starting transfers between devices  3.99 us (1%)
    all_gather x1, waiting for transfers between devices, per_device(): features = lax.all_gather(tokens, 'tp', axis=1, tiled=True)  48.5 us
    all_to_all x1, blocking collectives, per_device(): term = lax.all_to_all(term, 'loop', split_axis=0, concat_axis=1, tiled=True)  45.9 us
    reduce_scatter x1, waiting for transfers between devices, per_device(): input_grad = lax.psum_scatter(term, 'tp', scatter_dimension=1, tiled=True)  38.8 us
    all_gather x1, blocking collectives, per_device(): kind_of = lax.all_gather(own_kind, 'loop', axis=0, tiled=True)  32.2 us
    dot_general x3, matrix products, per_device(): jnp.dot(jnp.where(masks[kind], rows, 0), qkv_weight[kind], preferred_elem...  31.3 us
    dot_general x3, matrix products, per_device(): lax.dot_general(jnp.where(masks[kind], grads, 0), qkv_weight[kind], (((1,...  16.7 us
    dot_general x3, matrix products, per_device(): lax.dot_general(jnp.where(masks[kind], rows, 0), grads, (((0,), (0,)), ((...  13.6 us
    select_n x3, local copies, waits for them, and re-layouts, per_device(): jnp.where(masks[kind], rows, 0)  11.8 us
  transfers between devices with their start and end apart: 5, of which 2 were waited for; matrix products, arithmetic and copies ran while one was open for 33% of the time, Pallas kernels for 0%

commit v1 on v0

--- a/solution.py
+++ b/solution.py
@@ -28,7 +28,22 @@
             for kind in range(kinds)
         )
     ).astype(jnp.bfloat16)
-    term = lax.all_to_all(term, "loop", split_axis=0, concat_axis=1, tiled=True)
+    u_next = lax.psum(1, axis_name="loop")
+    part_next, base_arr = (u_next, lax.axis_index("loop"))
+    b_next = term.shape[0] // part_next
+    carry_in = list(term.shape)
+    carry_in[0] = b_next
+    after = carry_in[1]
+    carry_in[1] = after * part_next
+    q_next = jnp.zeros(carry_in, term.dtype)
+    for t in range(part_next):
+        t1 = lax.dynamic_slice_in_dim(term, (base_arr ^ t) * b_next, b_next, axis=0)
+        if t:
+            t1 = lax.ppermute(
+                t1, axis_name="loop", perm=tuple(((dev, dev ^ t) for dev in range(part_next)))
+            )
+        q_next = lax.dynamic_update_slice_in_dim(q_next, t1, (base_arr ^ t) * after, axis=1)
+    term = q_next
     input_grad = lax.psum_scatter(term, "tp", scatter_dimension=1, tiled=True)
     partial = sum(
         (

time: 279 us -> 280 us (level)
  blocking collectives: 78.1 us -> 32.3 us
  waiting for transfers between devices: 88.1 us -> 121 us
  local copies, waits for them, and re-layouts: 18.6 us -> 27.7 us
  starting transfers between devices: 3.99 us -> 8.34 us
    all_to_all x1 -> x0, blocking collectives: 45.9 us -> none  [per_device(): term = lax.all_to_all(term, 'loop', split_axis=0, concat_axis=1, tiled=True)]
    ppermute x0 -> x7, waiting for transfers between devices: none -> 30.5 us  [per_device(): lax.ppermute(t1, axis_name='loop', perm=tuple(((dev, dev ^ t) for dev in...]
    dynamic_update_slice x0 -> x7, local copies, waits for them, and re-layouts: none -> 8.16 us  [per_device(): lax.dynamic_update_slice_in_dim(q_next, t1, (base_arr ^ t) * after, axis=1)]
    ppermute x0 -> x7, starting transfers between devices: none -> 4.22 us  [per_device(): lax.ppermute(t1, axis_name='loop', perm=tuple(((dev, dev ^ t) for dev in...]
    reduce_scatter x1, waiting for transfers between devices: 38.8 us -> 41.7 us  [per_device(): input_grad = lax.psum_scatter(term, 'tp', scatter_dimension=1, tiled=True)]
  transfers between devices with their start and end apart: 5 -> 12, of which waited for: 2 -> 7; matrix products, arithmetic and copies ran while one was open for 33% -> 36% of each run, Pallas kernels for 0% -> 0%
where the time goes in v1:
time: 280 us; the launch traced here: 279 us
  waiting for transfers between devices  121 us (43%)
  matrix products  61.6 us (22%)
  blocking collectives  32.3 us (12%)
  local copies, waits for them, and re-layouts  27.7 us (10%)
  other arithmetic  14.1 us (5%)
  between operations  14 us (5%)
  starting transfers between devices  8.34 us (3%)
    all_gather x1, waiting for transfers between devices, per_device(): features = lax.all_gather(tokens, 'tp', axis=1, tiled=True)  48.5 us
    reduce_scatter x1, waiting for transfers between devices, per_device(): input_grad = lax.psum_scatter(term, 'tp', scatter_dimension=1, tiled=True)  41.7 us
    all_gather x1, blocking collectives, per_device(): kind_of = lax.all_gather(own_kind, 'loop', axis=0, tiled=True)  32.3 us
    dot_general x3, matrix products, per_device(): jnp.dot(jnp.where(masks[kind], rows, 0), qkv_weight[kind], preferred_elem...  31.3 us
    ppermute x7, waiting for transfers between devices, per_device(): lax.ppermute(t1, axis_name='loop', perm=tuple(((dev, dev ^ t) for dev in...  30.5 us
    dot_general x3, matrix products, per_device(): lax.dot_general(jnp.where(masks[kind], grads, 0), qkv_weight[kind], (((1,...  16.7 us
    dot_general x3, matrix products, per_device(): lax.dot_general(jnp.where(masks[kind], rows, 0), grads, (((0,), (0,)), ((...  13.6 us
    select_n x3, local copies, waits for them, and re-layouts, per_device(): jnp.where(masks[kind], rows, 0)  11.8 us
  transfers between devices with their start and end apart: 12, of which 7 were waited for; matrix products, arithmetic and copies ran while one was open for 36% of the time, Pallas kernels for 0%

profile of v1, /device:TPU:0, one launch (start us, length us, event | category | flops | bytes accessed | tf_op | source)
XLA Modules:
  0.0 279.5 jit_solution(1460138987989358045)
XLA Ops:
  7.2 0.0 all-gather.5.cloned.1.call-start
  7.2 2.0 copy.14
  9.3 0.0 all-gather.7.cloned.1.call-start
  9.3 0.7 all-gather.7.cloned.1.call-update
  10.0 48.5 %all-gather.5.cloned.1.call-done = bf16[256,4096]{0,1:T(8,128)(2,1)} async-done(((bf16[256,1024]{0,1:T(8,128)(2,1)}), bf16[256,4096]{0,1:T(8,128)(2,1)}) %all-gather.5.cloned.1.call-update) | async-done | bytes 2097168 | tf_op jit(solution)/shard_map/all_gather | solution.py:17
  58.5 3.8 %all-to-all-start = ((bf16[256,8,512]{0,2,1:T(8,128)(2,1)}), bf16[256,8,512]{0,2,1:T(8,128)(2,1)S(1)}, u32[]{:S(2)}, u32[]{:S(2)}) async-start(bf16[256,8,512]{0,2,1:T(8,128)(2,1)} %bitcast.62), calls=%async_computation | async-start | bytes 4194304 | tf_op jit(solution)/shard_map/all_to_all | solution.py:18
  62.3 0.0 reduce-scatter.3.cloned.1.call-start
  62.4 0.7 fusion.37
  63.1 5.0 %compare_select_fusion.1 = s32[256]{0:T(256)S(1)} fusion(s32[256]{0:T(256)S(1)} %copy-done.3, s32[]{:T(128)} %bitcast, s32[]{:T(128)} %bitcast.1, s32[]{:T(128)} %bitcast.2, s32[]{:T(128)} %bitcast.3, s32[]{:T(128)} %bitcast.4, s32[]{:T(128)} %bitcast.5, s32[]{:T(128)} %bitcast.6, s32[]{:T(128)} %bitcast.7), kind=kLoop, calls=%fused_computation.63 | loop fusion | flops 6400 | bytes 2080 | tf_op jit(solution)/shard_map/gather | solution.py:14
  68.1 32.3 %all-gather.1 = s32[8,1,256]{2,1,0:T(1,128)S(1)} all-gather(s32[1,1,256]{2,1,0:T(1,128)S(1)} %bitcast.68), channel_id=2, replica_groups=mesh['loop'=8,'tp'=4] {'loop'}, dimensions={0}, use_global_device_ids=true | all-gather | bytes 9216 | tf_op jit(solution)/shard_map/all_gather | solution.py:15
  100.4 2.9 %broadcast_select_fusion = (bf16[8,256,512]{1,2,0:T(8,128)(2,1)}, bf16[8,256,512]{1,2,0:T(8,128)(2,1)}, bf16[8,256,512]{1,2,0:T(8,128)(2,1)}) fusion(pred[8,256]{1,0:T(8,128)(4,1)S(1)} %bitcast.67, bf16[256,8,512]{0,2,1:T(8,128)(2,1)S(1)} %all-to-all-done, pred[8,256]{1,0:T(8,128)(4,1)S(1)} %bitcast.65, pred[8,256]{1,0:T(8,128)(4,1)S(1)} %bitcast.66), kind=kLoop, calls=%fused_computation.27 | loop fusion | flops 3145728 | bytes 8394752 | tf_op jit(solution)/shard_map/jit(_where)/select_n | solution.py:51
  103.3 3.9 %copy.15 = bf16[8,256,512]{2,1,0:T(8,128)(2,1)} copy(bf16[8,256,512]{1,2,0:T(8,128)(2,1)} %get-tuple-element.15) | data formatting | bytes 4194304 | tf_op jit(solution)/shard_map/jit(_where)/select_n | solution.py:51
  107.3 3.9 %copy.17 = bf16[8,256,512]{2,1,0:T(8,128)(2,1)} copy(bf16[8,256,512]{1,2,0:T(8,128)(2,1)} %get-tuple-element.16) | data formatting | bytes 4194304 | tf_op jit(solution)/shard_map/jit(_where)/select_n | solution.py:51
  111.2 3.9 %copy.19 = bf16[8,256,512]{2,1,0:T(8,128)(2,1)} copy(bf16[8,256,512]{1,2,0:T(8,128)(2,1)} %get-tuple-element.14) | data formatting | bytes 4194304 | tf_op jit(solution)/shard_map/jit(_where)/select_n | solution.py:51
  115.1 10.2 %fusion.26 = f32[2048,1536]{1,0:T(8,128)} fusion(bf16[2048,512]{1,0:T(8,128)(2,1)} %bitcast.63, bf16[3,512,1536]{2,1,0:T(8,128)(2,1)} %param.7), kind=kOutput, calls=%fused_computation.36 | convolution fusion | flops 3221225472 | bytes 16252928 | tf_op jit(solution)/shard_map/dot_general | solution.py:50
  125.3 7.9 %fusion.23 = f32[2048,1536]{1,0:T(8,128)} fusion(bf16[2048,512]{1,0:T(8,128)(2,1)S(1)} %bitcast.64, bf16[3,512,1536]{2,1,0:T(8,128)(2,1)} %param.7), kind=kOutput, calls=%fused_computation.33 | convolution fusion | flops 3221225472 | bytes 16252928 | tf_op jit(solution)/shard_map/dot_general | solution.py:50
  133.2 13.3 %add_convert_fusion = bf16[2048,1536]{1,0:T(8,128)(2,1)} fusion(f32[2048,1536]{1,0:T(8,128)} %fusion.26, f32[2048,1536]{1,0:T(8,128)} %fusion.23, bf16[2048,512]{1,0:T(8,128)(2,1)S(1)} %bitcast.61, bf16[3,512,1536]{2,1,0:T(8,128)(2,1)} %param.7), kind=kOutput, calls=%fused_computation | convolution fusion | flops 3230662656 | bytes 35127296 | tf_op jit(solution)/shard_map/dot_general | solution.py:50
  146.5 0.2 reduce-scatter.5.cloned.1.call-start
  146.8 0.0 all-gather.7.cloned.1.call-done
  146.8 6.3 %fusion = f32[2048,512]{1,0:T(8,128)S(1)} fusion(bf16[2048,1536]{1,0:T(8,128)(2,1)} %all-gather.7.cloned.1.call-done, pred[2048]{0:T(1024)(128)(4,1)S(1)} %reshape.54, bf16[3,512,1536]{2,1,0:T(8,128)(2,1)} %param.7), kind=kOutput, calls=%fused_computation.1 | convolution fusion | flops 3224371200 | bytes 12060672 | tf_op jit(solution)/shard_map/dot_general | solution.py:22
  153.1 5.2 %fusion.2 = f32[2048,512]{1,0:T(8,128)S(1)} fusion(bf16[2048,1536]{1,0:T(8,128)(2,1)S(1)} %copy-done.4, pred[2048]{0:T(1024)(128)(4,1)S(1)} %reshape.52, bf16[3,512,1536]{2,1,0:T(8,128)(2,1)} %param.7), kind=kOutput, calls=%fused_computation.3 | convolution fusion | flops 3224371200 | bytes 12060672 | tf_op jit(solution)/shard_map/dot_general | solution.py:22
  158.3 5.2 %add_convert_fusion.1 = bf16[2048,512]{1,0:T(8,128)(2,1)S(1)} fusion(f32[2048,512]{1,0:T(8,128)S(1)} %fusion, f32[2048,512]{1,0:T(8,128)S(1)} %fusion.2, bf16[2048,1536]{1,0:T(8,128)(2,1)S(1)} %copy-done.4, pred[2048]{0:T(1024)(128)(4,1)S(1)} %reshape.50, bf16[3,512,1536]{2,1,0:T(8,128)(2,1)} %param.7), kind=kOutput, calls=%fused_computation.11 | convolution fusion | flops 3227516928 | bytes 18352128 | tf_op jit(solution)/shard_map/dot_general | solution.py:22
  163.5 1.6 broadcast_in_dim.91
  165.1 1.0 constant_dynamic-slice_fusion
  166.1 0.2 collective-permute-start
  166.3 1.6 collective-permute-start.2
  168.0 0.7 collective-permute-start.3
  168.7 1.2 collective-permute-start.4
  169.8 0.5 collective-permute-start.5
  170.3 1.7 constant_dynamic-update-slice_fusion.5
  172.0 9.2 %collective-permute-done.1 = bf16[256,512]{1,0:T(8,128)(2,1)} collective-permute-done((bf16[256,512]{1,0:T(8,128)(2,1)}, bf16[256,512]{1,0:T(8,128)(2,1)}, u32[]{:S(2)}, u32[]{:S(2)}) %collective-permute-start.1) | collective-permute-done | bytes 262176 | tf_op jit(solution)/shard_map/ppermute | solution.py:42
  181.2 1.7 constant_dynamic-update-slice_fusion.4
  182.9 7.5 %collective-permute-done.2 = bf16[256,512]{1,0:T(8,128)(2,1)} collective-permute-done((bf16[256,512]{1,0:T(8,128)(2,1)S(1)}, bf16[256,512]{1,0:T(8,128)(2,1)}, u32[]{:S(2)}, u32[]{:S(2)}) %collective-permute-start.2) | collective-permute-done | bytes 262176 | tf_op jit(solution)/shard_map/ppermute | solution.py:42
  190.4 1.7 constant_dynamic-update-slice_fusion.3
  192.1 0.8 constant_dynamic-update-slice_fusion.2
  192.9 2.9 %collective-permute-done.4 = bf16[256,512]{1,0:T(8,128)(2,1)S(1)} collective-permute-done((bf16[256,512]{1,0:T(8,128)(2,1)S(1)}, bf16[256,512]{1,0:T(8,128)(2,1)S(1)}, u32[]{:S(2)}, u32[]{:S(2)}) %collective-permute-start.4) | collective-permute-done | bytes 262176 | tf_op jit(solution)/shard_map/ppermute | solution.py:42
  195.8 0.8 constant_dynamic-update-slice_fusion.1
  196.6 6.7 %collective-permute-done.5 = bf16[256,512]{1,0:T(8,128)(2,1)S(1)} collective-permute-done((bf16[256,512]{1,0:T(8,128)(2,1)S(1)}, bf16[256,512]{1,0:T(8,128)(2,1)S(1)}, u32[]{:S(2)}, u32[]{:S(2)}) %collective-permute-start.5) | collective-permute-done | bytes 262176 | tf_op jit(solution)/shard_map/ppermute | solution.py:42
  203.3 0.8 constant_dynamic-update-slice_fusion
  204.0 4.2 %collective-permute-done.6 = bf16[256,512]{1,0:T(8,128)(2,1)S(1)} collective-permute-done((bf16[256,512]{1,0:T(8,128)(2,1)S(1)}, bf16[256,512]{1,0:T(8,128)(2,1)S(1)}, u32[]{:S(2)}, u32[]{:S(2)}) %collective-permute-start.6) | collective-permute-done | bytes 262176 | tf_op jit(solution)/shard_map/ppermute | solution.py:42
  208.2 0.8 constant_dynamic-update-slice_fusion.6
  209.0 2.4 copy.20
  211.4 3.7 %bitcast_select_fusion.2 = (bf16[2048,512]{1,0:T(8,128)(2,1)S(1)}, bf16[2048,512]{1,0:T(8,128)(2,1)S(1)}, bf16[2048,512]{1,0:T(8,128)(2,1)S(1)}) fusion(bf16[8,256,512]{2,1,0:T(8,128)(2,1)} %copy.20, pred[2048]{0:T(1024)(128)(4,1)S(1)} %reshape.50, pred[2048]{0:T(1024)(128)(4,1)S(1)} %reshape.52, pred[2048]{0:T(1024)(128)(4,1)S(1)} %reshape.54), kind=kLoop, calls=%fused_computation.26 | loop fusion | flops 3145728 | bytes 8394752 | tf_op jit(solution)/shard_map/jit(_where)/select_n | solution.py:51
  215.1 6.5 %fusion.15 = bf16[1,512,1536]{2,1,0:T(8,128)(2,1)S(1)} fusion(bf16[2048,512]{1,0:T(8,128)(2,1)S(1)} %get-tuple-element.5, bf16[2048,1536]{1,0:T(8,128)(2,1)} %all-gather.7.cloned.1.call-done), kind=kOutput, calls=%fused_computation.21 | convolution fusion | flops 3222798336 | bytes 9961472 | tf_op jit(solution)/shard_map/dot_general | solution.py:62
  221.6 3.6 %fusion.16 = bf16[1,512,1536]{2,1,0:T(8,128)(2,1)S(1)} fusion(bf16[2048,512]{1,0:T(8,128)(2,1)S(1)} %get-tuple-element.4, bf16[2048,1536]{1,0:T(8,128)(2,1)S(1)} %bitcast.70), kind=kOutput, calls=%fused_computation.22 | convolution fusion | flops 3222798336 | bytes 9961472 | tf_op jit(solution)/shard_map/dot_general | solution.py:62
  225.2 3.6 %fusion.17 = bf16[1,512,1536]{2,1,0:T(8,128)(2,1)S(1)} fusion(bf16[2048,512]{1,0:T(8,128)(2,1)S(1)} %get-tuple-element.3, bf16[2048,1536]{1,0:T(8,128)(2,1)S(1)} %bitcast.70), kind=kOutput, calls=%fused_computation.23 | convolution fusion | flops 3222798336 | bytes 9961472 | tf_op jit(solution)/shard_map/dot_general | solution.py:62
  228.8 2.5 pad_maximum_fusion
  231.2 41.7 %reduce-scatter.5.cloned.1.call-done = bf16[256,1024]{1,0:T(8,128)(2,1)} async-done(((bf16[256,4096]{1,0:T(8,128)(2,1)}), bf16[256,1024]{1,0:T(8,128)(2,1)}) %reduce-scatter.5.cloned.1.call-update) | async-done | bytes 524304 | tf_op jit(solution)/shard_map/reduce_scatter | solution.py:47
  (28 shorter events, 0.1 us)
Async XLA Ops:
  7.2 51.4 %all-gather.5.cloned.1.call-start = ((), (), s32[]{:S(2)}) async-start(), calls=%async_computation.3 | async-start | bytes 2621440 | tf_op jit(solution)/shard_map/all_gather | solution.py:17
  9.3 137.5 %all-gather.7.cloned.1.call-start = ((), (), s32[]{:S(2)}) async-start(), calls=%async_computation.5 | async-start | bytes 7077888 | tf_op jit(solution)/shard_map/all_gather | solution.py:16
  58.5 3.8 %copy-start.2 = (s32[8]{0:T(128)S(1)}, s32[8]{0:T(128)}, u32[]{:S(2)}) copy-start(s32[8]{0:T(128)} %param.9) | copy-start | bytes 100
  58.5 4.5 %copy-start.3 = (s32[256]{0:T(256)S(1)}, s32[256]{0:T(256)}, u32[]{:S(2)}) copy-start(s32[256]{0:T(256)} %param.8) | copy-start | bytes 3076
  58.5 41.9 %all-to-all-start = ((bf16[256,8,512]{0,2,1:T(8,128)(2,1)}), bf16[256,8,512]{0,2,1:T(8,128)(2,1)S(1)}, u32[]{:S(2)}, u32[]{:S(2)}) async-start(bf16[256,8,512]{0,2,1:T(8,128)(2,1)} %bitcast.62), calls=%async_computation | async-start | bytes 4194304 | tf_op jit(solution)/shard_map/all_to_all | solution.py:18
  62.3 168.9 %reduce-scatter.3.cloned.1.call-start = ((), (), s32[]{:S(2)}) async-start(), calls=%async_computation.4 | async-start | bytes 7077888 | tf_op jit(solution)/shard_map/reduce_scatter | solution.py:58
  115.1 10.2 %copy-start.1 = (bf16[8,256,512]{2,1,0:T(8,128)(2,1)S(1)}, bf16[8,256,512]{2,1,0:T(8,128)(2,1)}, u32[]{:S(2)}) copy-start(bf16[8,256,512]{2,1,0:T(8,128)(2,1)} %copy.17) | copy-start | bytes 6291460
  125.3 7.9 %copy-start = (bf16[8,256,512]{2,1,0:T(8,128)(2,1)S(1)}, bf16[8,256,512]{2,1,0:T(8,128)(2,1)}, u32[]{:S(2)}) copy-start(bf16[8,256,512]{2,1,0:T(8,128)(2,1)} %copy.19) | copy-start | bytes 6291460
  146.5 126.5 %reduce-scatter.5.cloned.1.call-start = ((), (), s32[]{:S(2)}) async-start(), calls=%async_computation.6 | async-start | bytes 2621440 | tf_op jit(solution)/shard_map/reduce_scatter | solution.py:47
  146.8 6.3 %copy-start.4 = (bf16[2048,1536]{1,0:T(8,128)(2,1)S(1)}, bf16[2048,1536]{1,0:T(8,128)(2,1)}, u32[]{:S(2)}) copy-start(bf16[2048,1536]{1,0:T(8,128)(2,1)} %all-gather.7.cloned.1.call-done) | copy-start | bytes 18874372
  166.1 3.7 %collective-permute-start = (bf16[256,512]{1,0:T(8,128)(2,1)}, bf16[256,512]{1,0:T(8,128)(2,1)}, u32[]{:S(2)}, u32[]{:S(2)}) collective-permute-start(bf16[256,512]{1,0:T(8,128)(2,1)} %get-tuple-element.12), channel_id=1, source_target_pairs={{0,4},{4,0},{8,12},{12,8},{16,20},{20,16},{24,28},{28,24},{1,5},{5... | collective-permute-start | bytes 786440 | tf_op jit(solution)/shard_map/ppermute | solution.py:42
  166.3 14.9 %collective-permute-start.1 = (bf16[256,512]{1,0:T(8,128)(2,1)}, bf16[256,512]{1,0:T(8,128)(2,1)}, u32[]{:S(2)}, u32[]{:S(2)}) collective-permute-start(bf16[256,512]{1,0:T(8,128)(2,1)} %get-tuple-element.11), channel_id=1, source_target_pairs={{0,8},{4,12},{8,0},{12,4},{16,24},{20,28},{24,16},{28,20},{1,9},{5... | collective-permute-start | bytes 786440 | tf_op jit(solution)/shard_map/ppermute | solution.py:42
  166.3 24.1 %collective-permute-start.2 = (bf16[256,512]{1,0:T(8,128)(2,1)S(1)}, bf16[256,512]{1,0:T(8,128)(2,1)}, u32[]{:S(2)}, u32[]{:S(2)}) collective-permute-start(bf16[256,512]{1,0:T(8,128)(2,1)S(1)} %get-tuple-element.10), channel_id=1, source_target_pairs={{0,12},{4,8},{8,4},{12,0},{16,28},{20,24},{24,20},{28,16},{1,13},{... | collective-permute-start | bytes 786440 | tf_op jit(solution)/shard_map/ppermute | solution.py:42
  168.0 24.1 %collective-permute-start.3 = (bf16[256,512]{1,0:T(8,128)(2,1)S(1)}, bf16[256,512]{1,0:T(8,128)(2,1)S(1)}, u32[]{:S(2)}, u32[]{:S(2)}) collective-permute-start(bf16[256,512]{1,0:T(8,128)(2,1)S(1)} %get-tuple-element.9), channel_id=1, source_target_pairs={{0,16},{4,20},{8,24},{12,28},{16,0},{20,4},{24,8},{28,12},{1,17},{... | collective-permute-start | bytes 786440 | tf_op jit(solution)/shard_map/ppermute | solution.py:42
  168.7 27.2 %collective-permute-start.4 = (bf16[256,512]{1,0:T(8,128)(2,1)S(1)}, bf16[256,512]{1,0:T(8,128)(2,1)S(1)}, u32[]{:S(2)}, u32[]{:S(2)}) collective-permute-start(bf16[256,512]{1,0:T(8,128)(2,1)S(1)} %get-tuple-element.8), channel_id=1, source_target_pairs={{0,20},{4,16},{8,28},{12,24},{16,4},{20,0},{24,12},{28,8},{1,21},{... | collective-permute-start | bytes 786440 | tf_op jit(solution)/shard_map/ppermute | solution.py:42
  169.8 33.4 %collective-permute-start.5 = (bf16[256,512]{1,0:T(8,128)(2,1)S(1)}, bf16[256,512]{1,0:T(8,128)(2,1)S(1)}, u32[]{:S(2)}, u32[]{:S(2)}) collective-permute-start(bf16[256,512]{1,0:T(8,128)(2,1)S(1)} %get-tuple-element.7), channel_id=1, source_target_pairs={{0,24},{4,28},{8,16},{12,20},{16,8},{20,12},{24,0},{28,4},{1,25},{... | collective-permute-start | bytes 786440 | tf_op jit(solution)/shard_map/ppermute | solution.py:42
  181.2 27.0 %collective-permute-start.6 = (bf16[256,512]{1,0:T(8,128)(2,1)S(1)}, bf16[256,512]{1,0:T(8,128)(2,1)S(1)}, u32[]{:S(2)}, u32[]{:S(2)}) collective-permute-start(bf16[256,512]{1,0:T(8,128)(2,1)S(1)} %get-tuple-element.6), channel_id=1, source_target_pairs={{0,28},{4,24},{8,20},{12,16},{16,12},{20,8},{24,4},{28,0},{1,29},{... | collective-permute-start | bytes 786440 | tf_op jit(solution)/shard_map/ppermute | solution.py:42
  211.4 10.2 %slice-start = ((s8[6291456]{0:T(1024)(128)(4,1)}), s8[4194304]{0:T(1024)(128)(4,1)S(1)}, s32[]{:S(2)}) async-start(s8[6291456]{0:T(1024)(128)(4,1)} %bitcast.69), calls=%async_computation.7 | async-start | bytes 8388608
  215.1 6.5 %slice-start.1 = ((s8[6291456]{0:T(1024)(128)(4,1)}), s8[2097152]{0:T(1024)(128)(4,1)S(1)}, s32[]{:S(2)}) async-start(s8[6291456]{0:T(1024)(128)(4,1)} %bitcast.69), calls=%async_computation.8 | async-start | bytes 4194304
Sparse Core Ops, SparseCore 0:
  10.1 48.3 all-gather.4
  60.4 58.3 all-gather.6
  146.6 79.9 reduce-scatter.2
  229.3 43.6 reduce-scatter.4
